TPU v7x, 256 devices: a whole 4x4x8 slice. The times are simulated.
256 devices in a mesh: date: 16 (over x, y_hi, core), rng: 16 (over z, y_lo).
Axes of the slice: x: 4, y: 4 (y_hi: 2, y_lo: 2; y = y_hi * 2 + y_lo), z: 8, core: 2. Of those that a mesh axis runs over, the one named last changes fastest.
Arguments:
- slave_complex_pixels: bfloat16 [32, 2, 128, 4096], P(None, None, 'date', 'rng')
- along_track_line_groups: int32 [32, 16, 64], P(None, 'rng'), may hold values from 0 to 126, as said below
- master_epoch_position: int32 [1], replicated, may hold values from 0 to 31
- sweep_identifier: int32 [64], replicated, may hold values from 0 to 1, never falling along the last dimension, each value on 1 to 48 neighbouring positions
- initial_filter_kernel: float32 [32, 5, 3, 3], replicated, may hold values from -0.875 to 0.875
- initial_filter_shift: float32 [32], replicated, may hold values from -3 to 3
- latter_filter_kernel: float32 [2, 32, 3, 3], replicated, may hold values from -0.375 to 0.375
- latter_filter_shift: float32 [2], replicated, may hold values from -3 to 3
Outputs:
- burn_logits: float32 [32, 2, 64, 4096], P('date', None, None, 'rng')
Inputs may be any that keep to these rules, and one draw needn't show every extreme that they name: along_track_line_groups[d, g] is strictly increasing: the ingested rows that give the 64 window rows of date d in range segment g. `sweep_identifier`: burst never falls along the rows; each burst holds between 16 and 48 rows.
All inputs are finite; a program needn't handle non-finite values.
Results may differ from a plain program's by a relative error of at most 0.0003.
Values may be sent and summed in bfloat16 or wider, within the bound.
No kernel may reach another device: no remote copies, remote signals or barrier semaphores. Data moves between devices by JAX's collectives and lax.ppermute only.
A program may use at most 128 MiB of HBM per device.

v0:
```python
import jax
import jax.numpy as jnp
from jax import lax
from jax.sharding import PartitionSpec as P

BOX_AZ = 7
BOX_RG = 28
HIGH = lax.Precision.HIGHEST
EPSILON = 1e-06


def from_root(shard, axis, root):
    mine = lax.axis_index(axis) == root
    return lax.psum(jnp.where(mine, shard, jnp.zeros_like(shard)), axis)


def extended(shard, sides, width):
    for axis, dim in sides:
        devices, length = (lax.axis_size(axis), shard.shape[dim])
        up = [(i, (i + 1) % devices) for i in range(devices - 1)]
        down = [(j, i) for i, j in up]
        last = lax.slice_in_dim(shard, length - width, length, axis=dim)
        first = lax.slice_in_dim(shard, 0, width, axis=dim)
        before = lax.ppermute(last, axis, up)
        after = lax.ppermute(first, axis, down)
        shard = jnp.concatenate([before, shard, after], axis=dim)
    return shard


def pick_rows(one_frame, row_index):
    return jnp.take(one_frame, row_index, axis=1)


def features(moving_averaged):
    denominator = jnp.sqrt(moving_averaged[0] * moving_averaged[1]) + EPSILON
    return jnp.stack(
        [
            moving_averaged[2] / denominator,
            moving_averaged[3] / denominator,
            moving_averaged[4] / denominator,
            jnp.log(moving_averaged[1] + EPSILON) - jnp.log(moving_averaged[0] + EPSILON),
            jnp.log(moving_averaged[0] / (BOX_AZ * BOX_RG) + EPSILON),
        ]
    )


def range_band(padded_cols, result_across_lines):
    source_col = lax.broadcasted_iota(jnp.int32, (padded_cols, result_across_lines), 0)
    target_col = lax.broadcasted_iota(jnp.int32, (padded_cols, result_across_lines), 1)
    line_displacement = source_col - target_col
    return ((line_displacement >= 0) & (line_displacement < BOX_RG)).astype(jnp.float32)


def along_track_line_blocks(slant_averaged, sweep_identifier):
    along_track_lines_number = sweep_identifier.shape[0]
    block_line_number = min(128, along_track_lines_number)
    midway_line_number = (BOX_AZ - 1) // 2
    bordered_patch = jnp.pad(
        slant_averaged, ((0, 0), (0, 0), (midway_line_number, midway_line_number), (0, 0))
    )
    sweep_border_fill = jnp.pad(
        sweep_identifier, (midway_line_number, midway_line_number), constant_values=-1
    )
    patch_line_extent = block_line_number + 2 * midway_line_number
    target_row = lax.broadcasted_iota(jnp.int32, (block_line_number, patch_line_extent), 0)
    source_row = lax.broadcasted_iota(jnp.int32, (block_line_number, patch_line_extent), 1)
    near_rows = jnp.abs(source_row - midway_line_number - target_row) <= midway_line_number
    band_rows = (near_rows & (sweep_identifier[:, None] == sweep_border_fill[None, :])).astype(
        jnp.float32
    )
    results = jnp.einsum("pq,knqb->knpb", band_rows, bordered_patch, precision=HIGH)
    return results


def moving_average_planes(bordered_patch, sweep_identifier, result_across_lines):
    as_float = bordered_patch.astype(jnp.float32)
    ref_re = as_float[0, 0]
    ref_im = as_float[0, 1]
    sec_re = as_float[1:, 0]
    sec_im = as_float[1:, 1]
    pow_ref = jnp.broadcast_to(ref_re * ref_re + ref_im * ref_im, sec_re.shape)
    pow_sec = sec_re * sec_re + sec_im * sec_im
    cross_re = ref_re * sec_re + ref_im * sec_im
    cross_im = ref_im * sec_re - ref_re * sec_im
    layered_planes = jnp.stack([pow_ref, pow_sec, cross_re, cross_im, jnp.sqrt(pow_ref * pow_sec)])
    slant_averaged = jnp.einsum(
        "knpa,ab->knpb",
        layered_planes,
        range_band(bordered_patch.shape[3], result_across_lines),
        precision=HIGH,
    )
    moving_averaged = along_track_line_blocks(slant_averaged, sweep_identifier)
    return features(moving_averaged)


def conv_taps(field, weights, biases):
    along_track_lines_number = field.shape[2]
    across_track_number = field.shape[3] - 2
    bordered_patch = jnp.pad(field, ((0, 0), (0, 0), (1, 1), (0, 0)))
    cumulative_tally = (
        jnp.zeros(
            (weights.shape[0], field.shape[1], along_track_lines_number, across_track_number),
            jnp.float32,
        )
        + biases[:, None, None, None]
    )
    for tap_a in range(3):
        for tap_b in range(3):
            cumulative_tally = cumulative_tally + jnp.einsum(
                "oi,inpw->onpw",
                weights[:, :, tap_a, tap_b],
                bordered_patch[
                    :,
                    :,
                    tap_a : tap_a + along_track_lines_number,
                    tap_b : tap_b + across_track_number,
                ],
                precision=HIGH,
            )
    return cumulative_tally


def local(
    slave_complex_pixels,
    along_track_line_groups,
    master_epoch_position,
    sweep_identifier,
    initial_filter_kernel,
    initial_filter_shift,
    latter_filter_kernel,
    latter_filter_shift,
):
    date_count = lax.axis_size("date")
    date_index = lax.axis_index("date")
    per_dev = slave_complex_pixels.shape[0] // date_count
    across_track_number = slave_complex_pixels.shape[3]
    chosen = master_epoch_position[0]
    my_lists = along_track_line_groups[:, 0, :]
    lists_here = lax.dynamic_slice_in_dim(my_lists, date_index * per_dev, per_dev, 0)
    arrived = lax.all_to_all(slave_complex_pixels, "date", split_axis=0, concat_axis=2, tiled=True)
    secondary = jax.vmap(pick_rows)(arrived, lists_here)
    local_ref = lax.dynamic_index_in_dim(secondary, chosen % per_dev, 0, keepdims=False)
    ref_frame = from_root(local_ref, "date", chosen // per_dev)
    stacked = jnp.concatenate([ref_frame[None], secondary], 0)
    bordered_patch = extended(stacked, (("rng", 3),), BOX_RG // 2)
    descriptor_lattice = moving_average_planes(
        bordered_patch, sweep_identifier, across_track_number
    )
    descriptor_lattice = extended(descriptor_lattice, (("rng", 3),), 1)
    hidden = jax.nn.relu(conv_taps(descriptor_lattice, initial_filter_kernel, initial_filter_shift))
    hidden = extended(hidden, (("rng", 3),), 1)
    burn_logits = conv_taps(hidden, latter_filter_kernel, latter_filter_shift)
    return jnp.moveaxis(burn_logits, 0, 1)


def solution(mesh):
    placed = (P(None, None, "date", "rng"), P(None, "rng", None), P(), P(), P(), P(), P(), P())
    return jax.shard_map(
        local, mesh=mesh, in_specs=placed, out_specs=P("date", None, None, "rng"), check_vma=False
    )
```

profile of v0, /device:TPU:128, one launch (start us, length us, event | category | flops | bytes accessed | tf_op | source)
XLA Modules:
  0.0 294.7 jit_solution(7778671245150096637)
XLA Ops:
  6.5 7.2 %all-to-all-start = ((bf16[32,2,8,256]{3,2,1,0:T(8,128)(2,1)}), bf16[32,2,8,256]{3,2,1,0:T(8,128)(2,1)S(1)}, u32[]{:S(2)}, u32[]{:S(2)}) async-start(bf16[32,2,8,256]{3,2,1,0:T(8,128)(2,1)} %param.8), calls=%async_computation | async-start | bytes 524288 | tf_op jit(solution)/shard_map/all_to_all | solution.py:140
  15.5 7.4 %all-to-all-done = bf16[32,2,8,256]{3,2,1,0:T(8,128)(2,1)S(1)} async-done(((bf16[32,2,8,256]{3,2,1,0:T(8,128)(2,1)}), bf16[32,2,8,256]{3,2,1,0:T(8,128)(2,1)S(1)}, u32[]{:S(2)}, u32[]{:S(2)}) %all-to-all-start) | async-done | bytes 262176 | tf_op jit(solution)/shard_map/all_to_all | solution.py:140
  25.1 131.5 %all-reduce.6.cloned.1.call-done = bf16[1,2,64,256]{3,2,0,1:T(8,128)(2,1)} async-done(((bf16[1,2,64,256]{3,2,0,1:T(8,128)(2,1)}), bf16[1,2,64,256]{3,2,0,1:T(8,128)(2,1)}) %all-reduce.6.cloned.1.call-update) | async-done | bytes 65552 | tf_op jit(solution)/shard_map/psum | solution.py:14
  157.4 3.4 %collective-permute-start = (bf16[3,2,64,14]{3,2,0,1:T(8,128)(2,1)S(1)}, bf16[3,2,64,14]{3,2,0,1:T(8,128)(2,1)S(1)}, u32[]{:S(2)}, u32[]{:S(2)}) collective-permute-start(bf16[3,2,64,14]{3,2,0,1:T(8,128)(2,1)S(1)} %get-tuple-element.23), channel_id=1, source_target_pairs={{0,1},{1,2},{2,3},{3,4},{4,5},{5,6},{6,7},{7,8},{8,9},{9,10},{10,1... | collective-permute-start | bytes 32264 | tf_op jit(solution)/shard_map/ppermute | solution.py:24
  160.8 4.6 %collective-permute-start.1 = (bf16[3,2,64,14]{3,2,0,1:T(8,128)(2,1)S(1)}, bf16[3,2,64,14]{3,2,0,1:T(8,128)(2,1)S(1)}, u32[]{:S(2)}, u32[]{:S(2)}) collective-permute-start(bf16[3,2,64,14]{3,2,0,1:T(8,128)(2,1)S(1)} %get-tuple-element.24), channel_id=1, source_target_pairs={{1,0},{2,1},{3,2},{4,3},{5,4},{6,5},{7,6},{8,7},{9,8},{10,9},{11,1... | collective-permute-start | bytes 32264 | tf_op jit(solution)/shard_map/ppermute | solution.py:25
  170.6 3.2 %collective-permute-start.2 = (f32[5,2,64,1]{3,2,1,0:T(8,128)S(1)}, f32[5,2,64,1]{3,2,1,0:T(8,128)S(1)}, u32[]{:S(2)}, u32[]{:S(2)}) collective-permute-start(f32[5,2,64,1]{3,2,1,0:T(8,128)S(1)} %get-tuple-element.21), channel_id=1, source_target_pairs={{0,1},{1,2},{2,3},{3,4},{4,5},{5,6},{6,7},{7,8},{8,9},{9,10},{10,1... | collective-permute-start | bytes 7688 | tf_op jit(solution)/shard_map/ppermute | solution.py:24
  173.8 5.3 %collective-permute-start.3 = (f32[5,2,64,1]{3,2,1,0:T(8,128)S(1)}, f32[5,2,64,1]{3,2,1,0:T(8,128)S(1)}, u32[]{:S(2)}, u32[]{:S(2)}) collective-permute-start(f32[5,2,64,1]{3,2,1,0:T(8,128)S(1)} %get-tuple-element.22), channel_id=1, source_target_pairs={{1,0},{2,1},{3,2},{4,3},{5,4},{6,5},{7,6},{8,7},{9,8},{10,9},{11,1... | collective-permute-start | bytes 7688 | tf_op jit(solution)/shard_map/ppermute | solution.py:25
  179.1 3.6 %fusion.45 = f32[2,64,256,32]{2,3,1,0:T(8,128)S(1)} fusion(f32[5,2,64,256]{3,2,1,0:T(8,128)S(1)} %log_dynamic-update-slice_fusion, f32[32,5,1,1]{0,3,2,1:T(1,128)S(1)} %get-tuple-element.28), kind=kOutput, calls=%fused_computation.48 | convolution fusion | flops 62914560 | bytes 4850304 | tf_op jit(solution)/shard_map/oi,inpw->onpw/dot_general | solution.py:109
  184.8 3.9 %collective-permute-done.3 = f32[5,2,64,1]{3,2,1,0:T(8,128)S(1)} collective-permute-done((f32[5,2,64,1]{3,2,1,0:T(8,128)S(1)}, f32[5,2,64,1]{3,2,1,0:T(8,128)S(1)}, u32[]{:S(2)}, u32[]{:S(2)}) %collective-permute-start.3) | collective-permute-done | bytes 2592 | tf_op jit(solution)/shard_map/ppermute | solution.py:25
  190.0 3.6 %fusion.53 = f32[2,64,256,32]{2,3,1,0:T(8,128)S(1)} fusion(f32[5,2,64,256]{3,2,1,0:T(8,128)S(1)} %get-tuple-element.13, f32[32,5,1,1]{0,3,2,1:T(1,128)S(1)} %get-tuple-element.32), kind=kOutput, calls=%fused_computation.56 | convolution fusion | flops 62914560 | bytes 4850304 | tf_op jit(solution)/shard_map/oi,inpw->onpw/dot_general | solution.py:109
  193.5 3.6 %fusion.40 = f32[2,64,256,32]{2,3,1,0:T(8,128)S(1)} fusion(f32[5,2,64,256]{3,2,1,0:T(8,128)S(1)} %get-tuple-element.14, f32[32,5,1,1]{0,3,2,1:T(1,128)S(1)} %get-tuple-element.26), kind=kOutput, calls=%fused_computation.43 | convolution fusion | flops 62914560 | bytes 4850304 | tf_op jit(solution)/shard_map/oi,inpw->onpw/dot_general | solution.py:109
  197.1 5.3 %fusion.42 = f32[2,64,256,32]{2,3,1,0:T(8,128)} fusion(f32[5,2,64,256]{3,2,1,0:T(8,128)S(1)} %get-tuple-element.15, f32[32,5,1,1]{0,3,2,1:T(1,128)S(1)} %get-tuple-element.27), kind=kOutput, calls=%fused_computation.45 | convolution fusion | flops 62914560 | bytes 4850304 | tf_op jit(solution)/shard_map/oi,inpw->onpw/dot_general | solution.py:109
  202.4 5.0 %fusion.49 = f32[2,64,256,32]{2,3,1,0:T(8,128)} fusion(f32[5,2,64,256]{3,2,1,0:T(8,128)S(1)} %get-tuple-element.16, f32[32,5,1,1]{0,3,2,1:T(1,128)S(1)} %get-tuple-element.30), kind=kOutput, calls=%fused_computation.52 | convolution fusion | flops 62914560 | bytes 4850304 | tf_op jit(solution)/shard_map/oi,inpw->onpw/dot_general | solution.py:109
  207.5 5.1 %fusion.51 = f32[2,64,256,32]{2,3,1,0:T(8,128)} fusion(f32[5,2,64,256]{3,2,1,0:T(8,128)S(1)} %get-tuple-element.17, f32[32,5,1,1]{0,3,2,1:T(1,128)S(1)} %get-tuple-element.31), kind=kOutput, calls=%fused_computation.54 | convolution fusion | flops 62914560 | bytes 4850304 | tf_op jit(solution)/shard_map/oi,inpw->onpw/dot_general | solution.py:109
  212.5 5.0 %fusion.38 = f32[2,64,256,32]{2,3,1,0:T(8,128)} fusion(f32[5,2,64,256]{3,2,1,0:T(8,128)S(1)} %get-tuple-element.18, f32[32,5,1,1]{0,3,2,1:T(1,128)S(1)} %get-tuple-element.33), kind=kOutput, calls=%fused_computation.41 | convolution fusion | flops 62914560 | bytes 4850304 | tf_op jit(solution)/shard_map/oi,inpw->onpw/dot_general | solution.py:109
  218.1 5.0 %fusion.47 = f32[2,64,256,32]{2,3,1,0:T(8,128)} fusion(f32[5,2,64,256]{3,2,1,0:T(8,128)S(1)} %get-tuple-element.20, f32[32,5,1,1]{0,3,2,1:T(1,128)S(1)} %get-tuple-element.29), kind=kOutput, calls=%fused_computation.50 | convolution fusion | flops 62914560 | bytes 4850304 | tf_op jit(solution)/shard_map/oi,inpw->onpw/dot_general | solution.py:109
  223.1 10.2 %maximum_bitcast_fusion = f32[32,2,64,256]{3,0,2,1:T(8,128)S(1)} fusion(f32[2,64,256,32]{2,3,1,0:T(8,128)} %fusion.38, f32[2,64,256,32]{2,3,1,0:T(8,128)S(1)} %fusion.40, f32[2,64,256,32]{2,3,1,0:T(8,128)} %fusion.42, f32[2,64,256,32]{2,3,1,0:T(8,128)S(1)} %fusion.45, f32[2,64,256,32]{2,3,1,0:T(8,128)} %fusion.47, f32[2,64,256,32]{2,3,1,0:T(8,128)} %fusion.49, ...), kind=kOutput, calls=%fused_computation.24 | convolution fusion | flops 73400320 | bytes 38404864 | tf_op jit(solution)/shard_map/oi,inpw->onpw/dot_general | solution.py:109
  233.3 3.2 %fusion.114 = (f32[32,2,64,1]{3,0,2,1:T(8,128)}, f32[32,2,64,1]{3,0,2,1:T(8,128)}) fusion(f32[32,2,64,256]{3,0,2,1:T(8,128)S(1)} %maximum_bitcast_fusion), kind=kLoop, calls=%fused_computation.148 | loop fusion | bytes 65536 | tf_op jit(solution)/shard_map/slice | solution.py:22
  236.6 2.8 copy.95
  239.4 2.3 collective-permute-start.4
  241.7 4.5 %fusion.102 = f32[2,64,256,2]{2,3,1,0:T(2,128)S(1)} fusion(f32[32,2,64,256]{3,0,2,1:T(8,128)} %copy-done.2, f32[2,32,3,3]{1,0,3,2:T(2,128)S(1)} %copy-done.6), kind=kOutput, calls=%fused_computation.134 | convolution fusion | flops 25165824 | bytes 4457472 | tf_op jit(solution)/shard_map/oi,inpw->onpw/dot_general | solution.py:109
  247.3 6.0 %collective-permute-start.5 = (f32[32,2,64,1]{2,0,3,1:T(8,128)S(1)}, f32[32,2,64,1]{2,0,3,1:T(8,128)S(1)}, u32[]{:S(2)}, u32[]{:S(2)}) collective-permute-start(f32[32,2,64,1]{2,0,3,1:T(8,128)S(1)} %copy.96), channel_id=1, source_target_pairs={{1,0},{2,1},{3,2},{4,3},{5,4},{6,5},{7,6},{8,7},{9,8},{10,9},{11,1... | collective-permute-start | bytes 49160 | tf_op jit(solution)/shard_map/ppermute | solution.py:25
  255.2 4.9 %fusion.9 = f32[2,64,256,2]{2,3,1,0:T(2,128)S(1)} fusion(f32[32,2,64,256]{3,0,2,1:T(8,128)} %copy-done.2, f32[32,2,64,1]{3,0,2,1:T(8,128)S(1)} %copy.97, f32[2,32,3,3]{1,0,3,2:T(2,128)S(1)} %copy-done.6), kind=kOutput, calls=%fused_computation.16 | convolution fusion | flops 26214400 | bytes 6554624 | tf_op jit(solution)/shard_map/oi,inpw->onpw/dot_general | solution.py:109
  260.1 2.9 copy.98
  263.1 5.0 %select_maximum_fusion = f32[32,2,66,258]{3,0,2,1:T(8,128)S(1)} fusion(f32[32,2,64,1]{3,0,2,1:T(8,128)} %copy.98, f32[32,2,64,256]{3,0,2,1:T(8,128)} %copy-done.2, f32[32,2,64,1]{3,0,2,1:T(8,128)S(1)} %copy.97), kind=kLoop, calls=%fused_computation.3 | loop fusion | flops 8718336 | bytes 8586240 | tf_op jit(solution)/shard_map/concatenate | solution.py:26
  268.0 2.6 fusion.3
  270.7 2.3 fusion.5
  273.0 2.6 fusion.11
  275.6 2.6 fusion.13
  278.3 2.9 fusion.1
  281.2 2.4 fusion.34
  283.6 3.3 %fusion.27 = f32[2,2,64,256]{3,1,2,0:T(2,128)S(1)} fusion(f32[2,64,256,2]{2,3,1,0:T(2,128)S(1)} %fusion.1, f32[2,64,256,2]{2,3,1,0:T(2,128)S(1)} %fusion.3, f32[2,64,256,2]{2,3,1,0:T(2,128)S(1)} %fusion.5, f32[2,64,256,2]{2,3,1,0:T(2,128)S(1)} %fusion.34, f32[32,2,64,1]{3,0,2,1:T(8,128)S(1)} %copy-done.4, f32[32,2,64,256]{3,0,2,1:T(8,128)S(1)} %copy-done.3, ...), kind=kOutput, calls=%fused_computation.34 | convolution fusion | flops 26476544 | bytes 7603200 | tf_op jit(solution)/shard_map/oi,inpw->onpw/dot_general | solution.py:109
  (62 shorter events, 16.9 us)
Async XLA Ops:
  6.5 7.2 %copy-start = (s32[32,1,64]{2,1,0:T(1,128)S(1)}, s32[32,1,64]{2,1,0:T(1,128)}, u32[]{:S(2)}) copy-start(s32[32,1,64]{2,1,0:T(1,128)} %param.9) | copy-start | bytes 24580
  6.5 163.0 %copy-start.9 = (s32[64]{0:T(128)S(1)}, s32[64]{0:T(128)}, u32[]{:S(2)}) copy-start(s32[64]{0:T(128)} %param.11) | copy-start | bytes 772
  6.5 16.3 %all-to-all-start = ((bf16[32,2,8,256]{3,2,1,0:T(8,128)(2,1)}), bf16[32,2,8,256]{3,2,1,0:T(8,128)(2,1)S(1)}, u32[]{:S(2)}, u32[]{:S(2)}) async-start(bf16[32,2,8,256]{3,2,1,0:T(8,128)(2,1)} %param.8), calls=%async_computation | async-start | bytes 524288 | tf_op jit(solution)/shard_map/all_to_all | solution.py:140
  13.7 142.8 %all-reduce.6.cloned.1.call-start = ((), (), s32[]{:S(2)}) async-start(), calls=%async_computation.1 | async-start | bytes 131072 | tf_op jit(solution)/shard_map/psum | solution.py:14
  157.4 8.7 %collective-permute-start = (bf16[3,2,64,14]{3,2,0,1:T(8,128)(2,1)S(1)}, bf16[3,2,64,14]{3,2,0,1:T(8,128)(2,1)S(1)}, u32[]{:S(2)}, u32[]{:S(2)}) collective-permute-start(bf16[3,2,64,14]{3,2,0,1:T(8,128)(2,1)S(1)} %get-tuple-element.23), channel_id=1, source_target_pairs={{0,1},{1,2},{2,3},{3,4},{4,5},{5,6},{6,7},{7,8},{8,9},{9,10},{10,1... | collective-permute-start | bytes 32264 | tf_op jit(solution)/shard_map/ppermute | solution.py:24
  160.8 6.8 %collective-permute-start.1 = (bf16[3,2,64,14]{3,2,0,1:T(8,128)(2,1)S(1)}, bf16[3,2,64,14]{3,2,0,1:T(8,128)(2,1)S(1)}, u32[]{:S(2)}, u32[]{:S(2)}) collective-permute-start(bf16[3,2,64,14]{3,2,0,1:T(8,128)(2,1)S(1)} %get-tuple-element.24), channel_id=1, source_target_pairs={{1,0},{2,1},{3,2},{4,3},{5,4},{6,5},{7,6},{8,7},{9,8},{10,9},{11,1... | collective-permute-start | bytes 32264 | tf_op jit(solution)/shard_map/ppermute | solution.py:25
  170.6 14.2 %collective-permute-start.2 = (f32[5,2,64,1]{3,2,1,0:T(8,128)S(1)}, f32[5,2,64,1]{3,2,1,0:T(8,128)S(1)}, u32[]{:S(2)}, u32[]{:S(2)}) collective-permute-start(f32[5,2,64,1]{3,2,1,0:T(8,128)S(1)} %get-tuple-element.21), channel_id=1, source_target_pairs={{0,1},{1,2},{2,3},{3,4},{4,5},{5,6},{6,7},{7,8},{8,9},{9,10},{10,1... | collective-permute-start | bytes 7688 | tf_op jit(solution)/shard_map/ppermute | solution.py:24
  173.8 14.9 %collective-permute-start.3 = (f32[5,2,64,1]{3,2,1,0:T(8,128)S(1)}, f32[5,2,64,1]{3,2,1,0:T(8,128)S(1)}, u32[]{:S(2)}, u32[]{:S(2)}) collective-permute-start(f32[5,2,64,1]{3,2,1,0:T(8,128)S(1)} %get-tuple-element.22), channel_id=1, source_target_pairs={{1,0},{2,1},{3,2},{4,3},{5,4},{6,5},{7,6},{8,7},{9,8},{10,9},{11,1... | collective-permute-start | bytes 7688 | tf_op jit(solution)/shard_map/ppermute | solution.py:25
  217.6 5.5 %copy-start.7 = (f32[32]{0:T(128)S(1)}, f32[32]{0:T(128)}, u32[]{:S(2)}) copy-start(f32[32]{0:T(128)} %param.13) | copy-start | bytes 388
  233.3 3.3 %copy-start.2 = (f32[32,2,64,256]{3,0,2,1:T(8,128)}, f32[32,2,64,256]{3,0,2,1:T(8,128)S(1)}, u32[]{:S(2)}) copy-start(f32[32,2,64,256]{3,0,2,1:T(8,128)S(1)} %maximum_bitcast_fusion) | copy-start | bytes 12582916
  233.3 8.4 %copy-start.6 = (f32[2,32,3,3]{1,0,3,2:T(2,128)S(1)}, f32[2,32,3,3]{1,0,3,2:T(2,128)}, u32[]{:S(2)}) copy-start(f32[2,32,3,3]{1,0,3,2:T(2,128)} %param.14) | copy-start | bytes 6916
  236.6 9.6 %copy-start.5 = (f32[32,2,64,1]{3,0,2,1:T(8,128)S(1)}, f32[32,2,64,1]{3,0,2,1:T(8,128)}, u32[]{:S(2)}) copy-start(f32[32,2,64,1]{3,0,2,1:T(8,128)} %get-tuple-element.12) | copy-start | bytes 49156
  239.4 14.0 %collective-permute-start.4 = (f32[32,2,64,1]{2,0,3,1:T(8,128)S(1)}, f32[32,2,64,1]{2,0,3,1:T(8,128)S(1)}, u32[]{:S(2)}, u32[]{:S(2)}) collective-permute-start(f32[32,2,64,1]{2,0,3,1:T(8,128)S(1)} %copy.95), channel_id=1, source_target_pairs={{0,1},{1,2},{2,3},{3,4},{4,5},{5,6},{6,7},{7,8},{8,9},{9,10},{10,1... | collective-permute-start | bytes 49160 | tf_op jit(solution)/shard_map/ppermute | solution.py:24
  247.3 12.8 %collective-permute-start.5 = (f32[32,2,64,1]{2,0,3,1:T(8,128)S(1)}, f32[32,2,64,1]{2,0,3,1:T(8,128)S(1)}, u32[]{:S(2)}, u32[]{:S(2)}) collective-permute-start(f32[32,2,64,1]{2,0,3,1:T(8,128)S(1)} %copy.96), channel_id=1, source_target_pairs={{1,0},{2,1},{3,2},{4,3},{5,4},{6,5},{7,6},{8,7},{9,8},{10,9},{11,1... | collective-permute-start | bytes 49160 | tf_op jit(solution)/shard_map/ppermute | solution.py:25
  275.6 5.5 %copy-start.8 = (f32[2]{0:T(128)S(1)}, f32[2]{0:T(128)}, u32[]{:S(2)}) copy-start(f32[2]{0:T(128)} %param.15) | copy-start | bytes 28
  278.3 5.3 %copy-start.3 = (f32[32,2,64,256]{3,0,2,1:T(8,128)S(1)}, f32[32,2,64,256]{3,0,2,1:T(8,128)}, u32[]{:S(2)}) copy-start(f32[32,2,64,256]{3,0,2,1:T(8,128)} %copy-done.2) | copy-start | bytes 12582916
  278.3 5.3 %copy-start.4 = (f32[32,2,64,1]{3,0,2,1:T(8,128)S(1)}, f32[32,2,64,1]{3,0,2,1:T(8,128)}, u32[]{:S(2)}) copy-start(f32[32,2,64,1]{3,0,2,1:T(8,128)} %copy.98) | copy-start | bytes 49156
  281.2 6.5 %copy-start.1 = (s32[32,1,64]{2,1,0:T(1,128)S(1)}, s32[32,1,64]{2,1,0:T(1,128)}, u32[]{:S(2)}) copy-start(s32[32,1,64]{2,1,0:T(1,128)} %param.9) | copy-start | bytes 24580
Sparse Core Ops, SparseCore 0:
  25.1 131.4 all-reduce.5
where the time goes:
time: 299 us; the launch traced here: 295 us
  waiting for transfers between devices  146 us (49%)
  matrix products  75.8 us (25%)
  starting transfers between devices  32 us (11%)
  local copies, waits for them, and re-layouts  16.7 us (6%)
  between operations  14.8 us (5%)
  other arithmetic  9.08 us (3%)
    psum x1, waiting for transfers between devices, from_root(): return lax.psum(jnp.where(mine, shard, jnp.zeros_like(shard)), axis)  131 us
    dot_general x18, matrix products, conv_taps(): jnp.einsum('oi,inpw->onpw', weights[:, :, tap_a, tap_b], bordered_patch[:...  74.5 us
    ppermute x3, starting transfers between devices, extended(): after = lax.ppermute(first, axis, down)  15.9 us
    ppermute x3, starting transfers between devices, extended(): before = lax.ppermute(last, axis, up)  8.91 us
    all_to_all x1, waiting for transfers between devices, local(): lax.all_to_all(slave_complex_pixels, 'date', split_axis=0, concat_axis=2,...  7.41 us
    all_to_all x1, starting transfers between devices, local(): lax.all_to_all(slave_complex_pixels, 'date', split_axis=0, concat_axis=2,...  7.17 us
    slice x3, local copies, waits for them, and re-layouts, extended(): last = lax.slice_in_dim(shard, length - width, length, axis=dim)  6.1 us
  transfers between devices with their start and end apart: 8, of which 5 were waited for; matrix products, arithmetic and copies ran while one was open for 6% of the time, Pallas kernels for 0%

commit v1 on v0

--- a/solution.py
+++ b/solution.py
@@ -11,7 +11,7 @@
 
 def from_root(shard, axis, root):
     mine = lax.axis_index(axis) == root
-    return lax.psum(jnp.where(mine, shard, jnp.zeros_like(shard)), axis)
+    return jnp.sum(lax.all_gather(jnp.where(mine, shard, jnp.zeros_like(shard)), axis), axis=0)
 
 
 def extended(shard, sides, width):

time: 299 us -> 218 us (0.73)
  waiting for transfers between devices: 146 us -> 66.5 us
    psum x1 -> x0, waiting for transfers between devices: 131 us -> none  [from_root(): return lax.psum(jnp.where(mine, shard, jnp.zeros_like(shard)), axis)]
    all_gather x0 -> x1, waiting for transfers between devices: none -> 46.4 us  [from_root(): lax.all_gather(jnp.where(mine, shard, jnp.zeros_like(shard)), axis)]
    ppermute x3, waiting for transfers between devices: 2.13 us -> 5.61 us  [extended(): before = lax.ppermute(last, axis, up)]
  transfers between devices with their start and end apart: 8 -> 8, of which waited for: 5 -> 6; matrix products, arithmetic and copies ran while one was open for 6% -> 8% of each run, Pallas kernels for 0% -> 0%
where the time goes in v1:
time: 218 us; the launch traced here: 214 us
  matrix products  75.8 us (35%)
  waiting for transfers between devices  66.5 us (31%)
  starting transfers between devices  31.6 us (14%)
  local copies, waits for them, and re-layouts  16.1 us (7%)
  between operations  14.8 us (7%)
  other arithmetic  8.89 us (4%)
    dot_general x18, matrix products, conv_taps(): jnp.einsum('oi,inpw->onpw', weights[:, :, tap_a, tap_b], bordered_patch[:...  74.5 us
    all_gather x1, waiting for transfers between devices, from_root(): lax.all_gather(jnp.where(mine, shard, jnp.zeros_like(shard)), axis)  46.4 us
    ppermute x3, starting transfers between devices, extended(): after = lax.ppermute(first, axis, down)  17.3 us
    all_to_all x1, waiting for transfers between devices, local(): lax.all_to_all(slave_complex_pixels, 'date', split_axis=0, concat_axis=2,...  8.3 us
    all_to_all x1, starting transfers between devices, local(): lax.all_to_all(slave_complex_pixels, 'date', split_axis=0, concat_axis=2,...  7.17 us
    ppermute x3, starting transfers between devices, extended(): before = lax.ppermute(last, axis, up)  7.16 us
    ppermute x3, waiting for transfers between devices, extended(): after = lax.ppermute(first, axis, down)  6.13 us
    slice x3, local copies, waits for them, and re-layouts, extended(): last = lax.slice_in_dim(shard, length - width, length, axis=dim)  6.1 us
  transfers between devices with their start and end apart: 8, of which 6 were waited for; matrix products, arithmetic and copies ran while one was open for 8% of the time, Pallas kernels for 0%

profile of v1, /device:TPU:128, one launch (start us, length us, event | category | flops | bytes accessed | tf_op | source)
XLA Modules:
  0.0 213.6 jit_solution(9792612346393666871)
XLA Ops:
  6.5 7.2 %all-to-all-start = ((bf16[32,2,8,256]{3,2,1,0:T(8,128)(2,1)}), bf16[32,2,8,256]{3,2,1,0:T(8,128)(2,1)S(1)}, u32[]{:S(2)}, u32[]{:S(2)}) async-start(bf16[32,2,8,256]{3,2,1,0:T(8,128)(2,1)} %param.8), calls=%async_computation | async-start | bytes 524288 | tf_op jit(solution)/shard_map/all_to_all | solution.py:140
  14.6 8.3 %all-to-all-done = bf16[32,2,8,256]{3,2,1,0:T(8,128)(2,1)S(1)} async-done(((bf16[32,2,8,256]{3,2,1,0:T(8,128)(2,1)}), bf16[32,2,8,256]{3,2,1,0:T(8,128)(2,1)S(1)}, u32[]{:S(2)}, u32[]{:S(2)}) %all-to-all-start) | async-done | bytes 262176 | tf_op jit(solution)/shard_map/all_to_all | solution.py:140
  26.0 46.4 %all-gather.2.cloned.1.call-done = bf16[16,2,64,256]{3,2,0,1:T(8,128)(2,1)} async-done(((bf16[1,2,64,256]{3,2,0,1:T(8,128)(2,1)}), bf16[16,2,64,256]{3,2,0,1:T(8,128)(2,1)}) %all-gather.2.cloned.1.call-update) | async-done | bytes 1048592 | tf_op jit(solution)/shard_map/all_gather | solution.py:14
  73.8 2.5 %collective-permute-start = (bf16[3,2,64,14]{3,2,0,1:T(8,128)(2,1)S(1)}, bf16[3,2,64,14]{3,2,0,1:T(8,128)(2,1)S(1)}, u32[]{:S(2)}, u32[]{:S(2)}) collective-permute-start(bf16[3,2,64,14]{3,2,0,1:T(8,128)(2,1)S(1)} %get-tuple-element.23), channel_id=1, source_target_pairs={{0,1},{1,2},{2,3},{3,4},{4,5},{5,6},{6,7},{7,8},{8,9},{9,10},{10,1... | collective-permute-start | bytes 32264 | tf_op jit(solution)/shard_map/ppermute | solution.py:24
  76.3 5.5 %collective-permute-start.1 = (bf16[3,2,64,14]{3,2,0,1:T(8,128)(2,1)S(1)}, bf16[3,2,64,14]{3,2,0,1:T(8,128)(2,1)S(1)}, u32[]{:S(2)}, u32[]{:S(2)}) collective-permute-start(bf16[3,2,64,14]{3,2,0,1:T(8,128)(2,1)S(1)} %get-tuple-element.24), channel_id=1, source_target_pairs={{1,0},{2,1},{3,2},{4,3},{5,4},{6,5},{7,6},{8,7},{9,8},{10,9},{11,1... | collective-permute-start | bytes 32264 | tf_op jit(solution)/shard_map/ppermute | solution.py:25
  87.1 2.4 %collective-permute-start.2 = (f32[5,2,64,1]{3,2,1,0:T(8,128)S(1)}, f32[5,2,64,1]{3,2,1,0:T(8,128)S(1)}, u32[]{:S(2)}, u32[]{:S(2)}) collective-permute-start(f32[5,2,64,1]{3,2,1,0:T(8,128)S(1)} %get-tuple-element.21), channel_id=1, source_target_pairs={{0,1},{1,2},{2,3},{3,4},{4,5},{5,6},{6,7},{7,8},{8,9},{9,10},{10,1... | collective-permute-start | bytes 7688 | tf_op jit(solution)/shard_map/ppermute | solution.py:24
  89.4 5.8 %collective-permute-start.3 = (f32[5,2,64,1]{3,2,1,0:T(8,128)S(1)}, f32[5,2,64,1]{3,2,1,0:T(8,128)S(1)}, u32[]{:S(2)}, u32[]{:S(2)}) collective-permute-start(f32[5,2,64,1]{3,2,1,0:T(8,128)S(1)} %get-tuple-element.22), channel_id=1, source_target_pairs={{1,0},{2,1},{3,2},{4,3},{5,4},{6,5},{7,6},{8,7},{9,8},{10,9},{11,1... | collective-permute-start | bytes 7688 | tf_op jit(solution)/shard_map/ppermute | solution.py:25
  95.2 3.6 %fusion.45 = f32[2,64,256,32]{2,3,1,0:T(8,128)S(1)} fusion(f32[5,2,64,256]{3,2,1,0:T(8,128)S(1)} %log_dynamic-update-slice_fusion, f32[32,5,1,1]{0,3,2,1:T(1,128)S(1)} %get-tuple-element.28), kind=kOutput, calls=%fused_computation.48 | convolution fusion | flops 62914560 | bytes 4850304 | tf_op jit(solution)/shard_map/oi,inpw->onpw/dot_general | solution.py:109
  98.8 4.6 %collective-permute-done.2 = f32[5,2,64,1]{3,2,1,0:T(8,128)S(1)} collective-permute-done((f32[5,2,64,1]{3,2,1,0:T(8,128)S(1)}, f32[5,2,64,1]{3,2,1,0:T(8,128)S(1)}, u32[]{:S(2)}, u32[]{:S(2)}) %collective-permute-start.2) | collective-permute-done | bytes 2592 | tf_op jit(solution)/shard_map/ppermute | solution.py:24
  103.4 4.1 %collective-permute-done.3 = f32[5,2,64,1]{3,2,1,0:T(8,128)S(1)} collective-permute-done((f32[5,2,64,1]{3,2,1,0:T(8,128)S(1)}, f32[5,2,64,1]{3,2,1,0:T(8,128)S(1)}, u32[]{:S(2)}, u32[]{:S(2)}) %collective-permute-start.3) | collective-permute-done | bytes 2592 | tf_op jit(solution)/shard_map/ppermute | solution.py:25
  108.8 3.6 %fusion.53 = f32[2,64,256,32]{2,3,1,0:T(8,128)S(1)} fusion(f32[5,2,64,256]{3,2,1,0:T(8,128)S(1)} %get-tuple-element.13, f32[32,5,1,1]{0,3,2,1:T(1,128)S(1)} %get-tuple-element.32), kind=kOutput, calls=%fused_computation.56 | convolution fusion | flops 62914560 | bytes 4850304 | tf_op jit(solution)/shard_map/oi,inpw->onpw/dot_general | solution.py:109
  112.4 3.6 %fusion.40 = f32[2,64,256,32]{2,3,1,0:T(8,128)S(1)} fusion(f32[5,2,64,256]{3,2,1,0:T(8,128)S(1)} %get-tuple-element.14, f32[32,5,1,1]{0,3,2,1:T(1,128)S(1)} %get-tuple-element.26), kind=kOutput, calls=%fused_computation.43 | convolution fusion | flops 62914560 | bytes 4850304 | tf_op jit(solution)/shard_map/oi,inpw->onpw/dot_general | solution.py:109
  116.0 5.3 %fusion.42 = f32[2,64,256,32]{2,3,1,0:T(8,128)} fusion(f32[5,2,64,256]{3,2,1,0:T(8,128)S(1)} %get-tuple-element.15, f32[32,5,1,1]{0,3,2,1:T(1,128)S(1)} %get-tuple-element.27), kind=kOutput, calls=%fused_computation.45 | convolution fusion | flops 62914560 | bytes 4850304 | tf_op jit(solution)/shard_map/oi,inpw->onpw/dot_general | solution.py:109
  121.3 5.0 %fusion.49 = f32[2,64,256,32]{2,3,1,0:T(8,128)} fusion(f32[5,2,64,256]{3,2,1,0:T(8,128)S(1)} %get-tuple-element.16, f32[32,5,1,1]{0,3,2,1:T(1,128)S(1)} %get-tuple-element.30), kind=kOutput, calls=%fused_computation.52 | convolution fusion | flops 62914560 | bytes 4850304 | tf_op jit(solution)/shard_map/oi,inpw->onpw/dot_general | solution.py:109
  126.3 5.1 %fusion.51 = f32[2,64,256,32]{2,3,1,0:T(8,128)} fusion(f32[5,2,64,256]{3,2,1,0:T(8,128)S(1)} %get-tuple-element.17, f32[32,5,1,1]{0,3,2,1:T(1,128)S(1)} %get-tuple-element.31), kind=kOutput, calls=%fused_computation.54 | convolution fusion | flops 62914560 | bytes 4850304 | tf_op jit(solution)/shard_map/oi,inpw->onpw/dot_general | solution.py:109
  131.4 5.0 %fusion.38 = f32[2,64,256,32]{2,3,1,0:T(8,128)} fusion(f32[5,2,64,256]{3,2,1,0:T(8,128)S(1)} %get-tuple-element.18, f32[32,5,1,1]{0,3,2,1:T(1,128)S(1)} %get-tuple-element.33), kind=kOutput, calls=%fused_computation.41 | convolution fusion | flops 62914560 | bytes 4850304 | tf_op jit(solution)/shard_map/oi,inpw->onpw/dot_general | solution.py:109
  136.9 5.0 %fusion.47 = f32[2,64,256,32]{2,3,1,0:T(8,128)} fusion(f32[5,2,64,256]{3,2,1,0:T(8,128)S(1)} %get-tuple-element.20, f32[32,5,1,1]{0,3,2,1:T(1,128)S(1)} %get-tuple-element.29), kind=kOutput, calls=%fused_computation.50 | convolution fusion | flops 62914560 | bytes 4850304 | tf_op jit(solution)/shard_map/oi,inpw->onpw/dot_general | solution.py:109
  142.0 10.2 %maximum_bitcast_fusion = f32[32,2,64,256]{3,0,2,1:T(8,128)S(1)} fusion(f32[2,64,256,32]{2,3,1,0:T(8,128)} %fusion.38, f32[2,64,256,32]{2,3,1,0:T(8,128)S(1)} %fusion.40, f32[2,64,256,32]{2,3,1,0:T(8,128)} %fusion.42, f32[2,64,256,32]{2,3,1,0:T(8,128)S(1)} %fusion.45, f32[2,64,256,32]{2,3,1,0:T(8,128)} %fusion.47, f32[2,64,256,32]{2,3,1,0:T(8,128)} %fusion.49, ...), kind=kOutput, calls=%fused_computation.24 | convolution fusion | flops 73400320 | bytes 38404864 | tf_op jit(solution)/shard_map/oi,inpw->onpw/dot_general | solution.py:109
  152.2 3.2 %fusion.114 = (f32[32,2,64,1]{3,0,2,1:T(8,128)}, f32[32,2,64,1]{3,0,2,1:T(8,128)}) fusion(f32[32,2,64,256]{3,0,2,1:T(8,128)S(1)} %maximum_bitcast_fusion), kind=kLoop, calls=%fused_computation.148 | loop fusion | bytes 65536 | tf_op jit(solution)/shard_map/slice | solution.py:22
  155.5 2.8 %copy.95 = f32[32,2,64,1]{2,0,3,1:T(8,128)S(1)} copy(f32[32,2,64,1]{3,0,2,1:T(8,128)} %get-tuple-element.11) | data formatting | bytes 32768 | tf_op jit(solution)/shard_map/slice | solution.py:22
  160.6 4.5 %fusion.102 = f32[2,64,256,2]{2,3,1,0:T(2,128)S(1)} fusion(f32[32,2,64,256]{3,0,2,1:T(8,128)} %copy-done.2, f32[2,32,3,3]{1,0,3,2:T(2,128)S(1)} %copy-done.6), kind=kOutput, calls=%fused_computation.134 | convolution fusion | flops 25165824 | bytes 4457472 | tf_op jit(solution)/shard_map/oi,inpw->onpw/dot_general | solution.py:109
  166.2 6.0 %collective-permute-start.5 = (f32[32,2,64,1]{2,0,3,1:T(8,128)S(1)}, f32[32,2,64,1]{2,0,3,1:T(8,128)S(1)}, u32[]{:S(2)}, u32[]{:S(2)}) collective-permute-start(f32[32,2,64,1]{2,0,3,1:T(8,128)S(1)} %copy.96), channel_id=1, source_target_pairs={{1,0},{2,1},{3,2},{4,3},{5,4},{6,5},{7,6},{8,7},{9,8},{10,9},{11,1... | collective-permute-start | bytes 49160 | tf_op jit(solution)/shard_map/ppermute | solution.py:25
  174.1 4.9 %fusion.9 = f32[2,64,256,2]{2,3,1,0:T(2,128)S(1)} fusion(f32[32,2,64,256]{3,0,2,1:T(8,128)} %copy-done.2, f32[32,2,64,1]{3,0,2,1:T(8,128)S(1)} %copy.97, f32[2,32,3,3]{1,0,3,2:T(2,128)S(1)} %copy-done.6), kind=kOutput, calls=%fused_computation.16 | convolution fusion | flops 26214400 | bytes 6554624 | tf_op jit(solution)/shard_map/oi,inpw->onpw/dot_general | solution.py:109
  179.0 2.9 %copy.98 = f32[32,2,64,1]{3,0,2,1:T(8,128)} copy(f32[32,2,64,1]{2,0,3,1:T(8,128)S(1)} %collective-permute-done.5) | data formatting | bytes 32768 | tf_op jit(solution)/shard_map/ppermute | solution.py:25
  181.9 5.0 %select_maximum_fusion = f32[32,2,66,258]{3,0,2,1:T(8,128)S(1)} fusion(f32[32,2,64,1]{3,0,2,1:T(8,128)} %copy.98, f32[32,2,64,256]{3,0,2,1:T(8,128)} %copy-done.2, f32[32,2,64,1]{3,0,2,1:T(8,128)S(1)} %copy.97), kind=kLoop, calls=%fused_computation.3 | loop fusion | flops 8718336 | bytes 8586240 | tf_op jit(solution)/shard_map/concatenate | solution.py:26
  186.9 2.6 %fusion.3 = f32[2,64,256,2]{2,3,1,0:T(2,128)S(1)} fusion(f32[32,2,66,258]{3,0,2,1:T(8,128)S(1)} %select_maximum_fusion, f32[2,32,3,3]{1,0,3,2:T(2,128)S(1)} %copy-done.6), kind=kOutput, calls=%fused_computation.8 | convolution fusion | flops 25165824 | bytes 4457472 | tf_op jit(solution)/shard_map/oi,inpw->onpw/dot_general | solution.py:109
  189.5 2.3 %fusion.5 = f32[2,64,256,2]{2,3,1,0:T(2,128)S(1)} fusion(f32[32,2,66,258]{3,0,2,1:T(8,128)S(1)} %select_maximum_fusion, f32[2,32,3,3]{1,0,3,2:T(2,128)S(1)} %copy-done.6), kind=kOutput, calls=%fused_computation.10 | convolution fusion | flops 25165824 | bytes 4457472 | tf_op jit(solution)/shard_map/oi,inpw->onpw/dot_general | solution.py:109
  191.9 2.6 %fusion.11 = f32[2,64,256,2]{2,3,1,0:T(2,128)S(1)} fusion(f32[32,2,66,258]{3,0,2,1:T(8,128)S(1)} %select_maximum_fusion, f32[2,32,3,3]{1,0,3,2:T(2,128)S(1)} %copy-done.6), kind=kOutput, calls=%fused_computation.18 | convolution fusion | flops 25165824 | bytes 4457472 | tf_op jit(solution)/shard_map/oi,inpw->onpw/dot_general | solution.py:109
  194.5 2.6 %fusion.13 = f32[2,64,256,2]{2,3,1,0:T(2,128)S(1)} fusion(f32[32,2,66,258]{3,0,2,1:T(8,128)S(1)} %select_maximum_fusion, f32[2,32,3,3]{1,0,3,2:T(2,128)S(1)} %copy-done.6), kind=kOutput, calls=%fused_computation.20 | convolution fusion | flops 25165824 | bytes 4457472 | tf_op jit(solution)/shard_map/oi,inpw->onpw/dot_general | solution.py:109
  197.2 2.9 %fusion.1 = f32[2,64,256,2]{2,3,1,0:T(2,128)S(1)} fusion(f32[32,2,66,258]{3,0,2,1:T(8,128)S(1)} %select_maximum_fusion, f32[2,32,3,3]{1,0,3,2:T(2,128)S(1)} %copy-done.6), kind=kOutput, calls=%fused_computation.6 | convolution fusion | flops 25165824 | bytes 4457472 | tf_op jit(solution)/shard_map/oi,inpw->onpw/dot_general | solution.py:109
  200.1 2.4 %fusion.34 = f32[2,64,256,2]{2,3,1,0:T(2,128)S(1)} fusion(f32[2,64,256,2]{2,3,1,0:T(2,128)S(1)} %fusion.102, f32[2,64,256,2]{2,3,1,0:T(2,128)S(1)} %fusion.9, f32[2,64,256,2]{2,3,1,0:T(2,128)S(1)} %fusion.11, f32[2,64,256,2]{2,3,1,0:T(2,128)S(1)} %fusion.13, f32[32,2,66,258]{3,0,2,1:T(8,128)S(1)} %select_maximum_fusion, f32[2]{0:T(128)S(1)} %copy-done.8, ...), kind=kOutput, calls=%fused_computation.37 | convolution fusion | flops 25493504 | bytes 5506560 | tf_op jit(solution)/shard_map/oi,inpw->onpw/dot_general | solution.py:109
  202.5 3.3 %fusion.27 = f32[2,2,64,256]{3,1,2,0:T(2,128)S(1)} fusion(f32[2,64,256,2]{2,3,1,0:T(2,128)S(1)} %fusion.1, f32[2,64,256,2]{2,3,1,0:T(2,128)S(1)} %fusion.3, f32[2,64,256,2]{2,3,1,0:T(2,128)S(1)} %fusion.5, f32[2,64,256,2]{2,3,1,0:T(2,128)S(1)} %fusion.34, f32[32,2,64,1]{3,0,2,1:T(8,128)S(1)} %copy-done.4, f32[32,2,64,256]{3,0,2,1:T(8,128)S(1)} %copy-done.3, ...), kind=kOutput, calls=%fused_computation.34 | convolution fusion | flops 26476544 | bytes 7603200 | tf_op jit(solution)/shard_map/oi,inpw->onpw/dot_general | solution.py:109
  (63 shorter events, 17.7 us)
Async XLA Ops:
  6.5 7.2 %copy-start = (s32[32,1,64]{2,1,0:T(1,128)S(1)}, s32[32,1,64]{2,1,0:T(1,128)}, u32[]{:S(2)}) copy-start(s32[32,1,64]{2,1,0:T(1,128)} %param.9) | copy-start | bytes 24580
  6.5 75.3 %copy-start.9 = (s32[64]{0:T(128)S(1)}, s32[64]{0:T(128)}, u32[]{:S(2)}) copy-start(s32[64]{0:T(128)} %param.11) | copy-start | bytes 772
  6.5 16.3 %all-to-all-start = ((bf16[32,2,8,256]{3,2,1,0:T(8,128)(2,1)}), bf16[32,2,8,256]{3,2,1,0:T(8,128)(2,1)S(1)}, u32[]{:S(2)}, u32[]{:S(2)}) async-start(bf16[32,2,8,256]{3,2,1,0:T(8,128)(2,1)} %param.8), calls=%async_computation | async-start | bytes 524288 | tf_op jit(solution)/shard_map/all_to_all | solution.py:140
  13.7 58.7 %all-gather.2.cloned.1.call-start = ((), (), s32[]{:S(2)}) async-start(), calls=%async_computation.1 | async-start | bytes 1114112 | tf_op jit(solution)/shard_map/all_gather | solution.py:14
  73.8 9.0 %collective-permute-start = (bf16[3,2,64,14]{3,2,0,1:T(8,128)(2,1)S(1)}, bf16[3,2,64,14]{3,2,0,1:T(8,128)(2,1)S(1)}, u32[]{:S(2)}, u32[]{:S(2)}) collective-permute-start(bf16[3,2,64,14]{3,2,0,1:T(8,128)(2,1)S(1)} %get-tuple-element.23), channel_id=1, source_target_pairs={{0,1},{1,2},{2,3},{3,4},{4,5},{5,6},{6,7},{7,8},{8,9},{9,10},{10,1... | collective-permute-start | bytes 32264 | tf_op jit(solution)/shard_map/ppermute | solution.py:24
  76.3 8.5 %collective-permute-start.1 = (bf16[3,2,64,14]{3,2,0,1:T(8,128)(2,1)S(1)}, bf16[3,2,64,14]{3,2,0,1:T(8,128)(2,1)S(1)}, u32[]{:S(2)}, u32[]{:S(2)}) collective-permute-start(bf16[3,2,64,14]{3,2,0,1:T(8,128)(2,1)S(1)} %get-tuple-element.24), channel_id=1, source_target_pairs={{1,0},{2,1},{3,2},{4,3},{5,4},{6,5},{7,6},{8,7},{9,8},{10,9},{11,1... | collective-permute-start | bytes 32264 | tf_op jit(solution)/shard_map/ppermute | solution.py:25
  87.1 16.4 %collective-permute-start.2 = (f32[5,2,64,1]{3,2,1,0:T(8,128)S(1)}, f32[5,2,64,1]{3,2,1,0:T(8,128)S(1)}, u32[]{:S(2)}, u32[]{:S(2)}) collective-permute-start(f32[5,2,64,1]{3,2,1,0:T(8,128)S(1)} %get-tuple-element.21), channel_id=1, source_target_pairs={{0,1},{1,2},{2,3},{3,4},{4,5},{5,6},{6,7},{7,8},{8,9},{9,10},{10,1... | collective-permute-start | bytes 7688 | tf_op jit(solution)/shard_map/ppermute | solution.py:24
  89.4 18.1 %collective-permute-start.3 = (f32[5,2,64,1]{3,2,1,0:T(8,128)S(1)}, f32[5,2,64,1]{3,2,1,0:T(8,128)S(1)}, u32[]{:S(2)}, u32[]{:S(2)}) collective-permute-start(f32[5,2,64,1]{3,2,1,0:T(8,128)S(1)} %get-tuple-element.22), channel_id=1, source_target_pairs={{1,0},{2,1},{3,2},{4,3},{5,4},{6,5},{7,6},{8,7},{9,8},{10,9},{11,1... | collective-permute-start | bytes 7688 | tf_op jit(solution)/shard_map/ppermute | solution.py:25
  136.4 5.5 %copy-start.7 = (f32[32]{0:T(128)S(1)}, f32[32]{0:T(128)}, u32[]{:S(2)}) copy-start(f32[32]{0:T(128)} %param.13) | copy-start | bytes 388
  152.2 3.3 %copy-start.2 = (f32[32,2,64,256]{3,0,2,1:T(8,128)}, f32[32,2,64,256]{3,0,2,1:T(8,128)S(1)}, u32[]{:S(2)}) copy-start(f32[32,2,64,256]{3,0,2,1:T(8,128)S(1)} %maximum_bitcast_fusion) | copy-start | bytes 12582916
  152.2 8.4 %copy-start.6 = (f32[2,32,3,3]{1,0,3,2:T(2,128)S(1)}, f32[2,32,3,3]{1,0,3,2:T(2,128)}, u32[]{:S(2)}) copy-start(f32[2,32,3,3]{1,0,3,2:T(2,128)} %param.14) | copy-start | bytes 6916
  155.5 9.6 %copy-start.5 = (f32[32,2,64,1]{3,0,2,1:T(8,128)S(1)}, f32[32,2,64,1]{3,0,2,1:T(8,128)}, u32[]{:S(2)}) copy-start(f32[32,2,64,1]{3,0,2,1:T(8,128)} %get-tuple-element.12) | copy-start | bytes 49156
  158.3 14.0 %collective-permute-start.4 = (f32[32,2,64,1]{2,0,3,1:T(8,128)S(1)}, f32[32,2,64,1]{2,0,3,1:T(8,128)S(1)}, u32[]{:S(2)}, u32[]{:S(2)}) collective-permute-start(f32[32,2,64,1]{2,0,3,1:T(8,128)S(1)} %copy.95), channel_id=1, source_target_pairs={{0,1},{1,2},{2,3},{3,4},{4,5},{5,6},{6,7},{7,8},{8,9},{9,10},{10,1... | collective-permute-start | bytes 49160 | tf_op jit(solution)/shard_map/ppermute | solution.py:24
  166.2 12.8 %collective-permute-start.5 = (f32[32,2,64,1]{2,0,3,1:T(8,128)S(1)}, f32[32,2,64,1]{2,0,3,1:T(8,128)S(1)}, u32[]{:S(2)}, u32[]{:S(2)}) collective-permute-start(f32[32,2,64,1]{2,0,3,1:T(8,128)S(1)} %copy.96), channel_id=1, source_target_pairs={{1,0},{2,1},{3,2},{4,3},{5,4},{6,5},{7,6},{8,7},{9,8},{10,9},{11,1... | collective-permute-start | bytes 49160 | tf_op jit(solution)/shard_map/ppermute | solution.py:25
  194.5 5.5 %copy-start.8 = (f32[2]{0:T(128)S(1)}, f32[2]{0:T(128)}, u32[]{:S(2)}) copy-start(f32[2]{0:T(128)} %param.15) | copy-start | bytes 28
  197.2 5.3 %copy-start.3 = (f32[32,2,64,256]{3,0,2,1:T(8,128)S(1)}, f32[32,2,64,256]{3,0,2,1:T(8,128)}, u32[]{:S(2)}) copy-start(f32[32,2,64,256]{3,0,2,1:T(8,128)} %copy-done.2) | copy-start | bytes 12582916
  197.2 5.3 %copy-start.4 = (f32[32,2,64,1]{3,0,2,1:T(8,128)S(1)}, f32[32,2,64,1]{3,0,2,1:T(8,128)}, u32[]{:S(2)}) copy-start(f32[32,2,64,1]{3,0,2,1:T(8,128)} %copy.98) | copy-start | bytes 49156
  200.1 6.5 %copy-start.1 = (s32[32,1,64]{2,1,0:T(1,128)S(1)}, s32[32,1,64]{2,1,0:T(1,128)}, u32[]{:S(2)}) copy-start(s32[32,1,64]{2,1,0:T(1,128)} %param.9) | copy-start | bytes 24580
Sparse Core Ops, SparseCore 0:
  25.1 47.2 all-gather.1
